TPU v7x, 32 devices: a whole 2x2x4 slice. The times are simulated.
32 devices in a mesh: tm: 2 (over y), obs: 16 (over z, x, core).
Axes of the slice: x: 2, y: 2, z: 4, core: 2. Of those that a mesh axis runs over, the one named last changes fastest.
Arguments:
- flux: bfloat16 [4, 64, 16384], P('tm', 'obs'), may hold values from -6 to 6
- footprint: bfloat16 [2048, 16384], P(('tm', 'obs')), may hold values from -0.046875 to 0.046875
- entry_owner: int32 [2048, 1], P(('tm', 'obs')), may hold values from 0 to 15; in each aligned block of 64 rows (0 to 63, 64 to 127, ...) at most 8 rows name the same one
- entry_tile: int32 [32, 64], P(('tm', 'obs')), may hold values from 0 to 3
- entry_lag: int32 [32, 64], P(('tm', 'obs')), may hold values from 0 to 1
- entry_sounding: int32 [32, 64], P(('tm', 'obs')), may hold values from 0 to 15, never falling along the last dimension, each value on 1 to 8 neighbouring positions
- sounding_window: int32 [32, 16], P(('tm', 'obs')), may hold values from 1 to 3
- observed: float32 [32, 16], P(('tm', 'obs')), may hold values from -8 to 8
- obs_weight: float32 [32, 16], P(('tm', 'obs')), may hold values from 0.25 to 4
Outputs:
- modeled: float32 [32, 16], P(('tm', 'obs'))
- gradient: float32 [4, 64, 16384], P('tm', 'obs')
Inputs may be any that keep to these rules, and one draw needn't show every extreme that they name: `entry_owner`: among the 64 entries of one device no owner is named more than 8 times, and on some device some owner is named exactly 8 times.
All inputs are finite; a program needn't handle non-finite values.
Results may differ from a plain program's by a relative error of at most 0.0029.
Values may be sent and summed in bfloat16 or wider, within the bound.
A program may use at most 64 MiB of HBM per device.

v0:
```python
import jax
import jax.numpy as jnp
from jax import lax
from jax.sharding import PartitionSpec as P


def per_device(
    flux,
    footprint,
    entry_owner,
    entry_tile,
    entry_lag,
    entry_sounding,
    sounding_window,
    observed,
    obs_weight,
):
    peer_count = lax.axis_size("obs")
    entry_count = footprint.shape[0]
    cell_count = footprint.shape[1]
    tile_dev = flux.shape[1]
    sounding_count = observed.shape[1]
    slot_cap = 2 * entry_count // peer_count
    owners = entry_owner[:, 0]
    sounding = entry_sounding[0]
    sounding_hot = sounding[:, None] == jnp.arange(sounding_count, dtype=jnp.int32)[None, :]
    window = jnp.sum(jnp.where(sounding_hot, sounding_window[0][None, :], 0), axis=1) - entry_lag[0]
    target = window * tile_dev + entry_tile[0]
    owner_hot = (owners[:, None] == jnp.arange(peer_count, dtype=jnp.int32)[None, :]).astype(
        jnp.int32
    )
    rank_within = jnp.sum((jnp.cumsum(owner_hot, axis=0) - owner_hot) * owner_hot, axis=1)
    slot_index = owners * slot_cap + rank_within
    send_blocks = (
        jnp.zeros((peer_count * slot_cap, cell_count), jnp.bfloat16).at[slot_index].set(footprint)
    )
    send_blocks = send_blocks.reshape(peer_count, slot_cap, cell_count)
    send_target = jnp.zeros((peer_count * slot_cap,), jnp.int32).at[slot_index].set(target)
    send_target = send_target.reshape(peer_count, slot_cap)
    everything = lax.all_gather(flux, "tm", axis=0, tiled=True).reshape(-1, cell_count)
    got_blocks, got_target = (
        lax.all_to_all(send_blocks, "obs", split_axis=0, concat_axis=0, tiled=True),
        lax.all_to_all(send_target, "obs", split_axis=0, concat_axis=0, tiled=True),
    )
    selected = everything[got_target.reshape(-1)].reshape(got_blocks.shape)
    returned = lax.all_to_all(
        jnp.einsum("pkc,pkc->pk", got_blocks, selected, preferred_element_type=jnp.float32),
        "obs",
        split_axis=0,
        concat_axis=0,
        tiled=True,
    )
    entry_dots = returned.reshape(-1)[slot_index]
    modeled = jnp.sum(jnp.where(sounding_hot, entry_dots[:, None], 0.0), axis=0)
    residual = obs_weight[0] * (modeled - observed[0])
    entry_resid = jnp.sum(jnp.where(sounding_hot, residual[None, :], 0.0), axis=1)
    slot_resid = jnp.zeros((peer_count * slot_cap,), jnp.float32).at[slot_index].set(entry_resid)
    got_resid = lax.all_to_all(
        slot_resid.reshape(peer_count, slot_cap), "obs", split_axis=0, concat_axis=0, tiled=True
    )
    contribution = (got_resid[:, :, None] * got_blocks).astype(jnp.bfloat16)
    targets = got_target
    contribution = contribution.reshape(-1, cell_count)
    targets = targets.reshape(-1)
    row_count = flux.shape[0] * lax.axis_size("tm")
    row_ids = jnp.arange(row_count * tile_dev, dtype=jnp.int32)
    row_match = (row_ids[:, None] == targets[None, :]).astype(jnp.bfloat16)
    summed = jnp.dot(row_match, contribution, preferred_element_type=jnp.float32)
    gradient = lax.psum_scatter(
        summed.reshape(row_count, tile_dev * cell_count), "tm", scatter_dimension=0, tiled=True
    )
    gradient = gradient.reshape(flux.shape[0], tile_dev, cell_count)
    return (modeled[None, :], gradient)


def solution(mesh):
    placed = (
        P("tm", "obs", None),
        P(("tm", "obs"), None),
        P(("tm", "obs"), None),
        P(("tm", "obs"), None),
        P(("tm", "obs"), None),
        P(("tm", "obs"), None),
        P(("tm", "obs"), None),
        P(("tm", "obs"), None),
        P(("tm", "obs"), None),
    )
    return jax.shard_map(
        per_device,
        mesh=mesh,
        in_specs=placed,
        out_specs=(P(("tm", "obs"), None), P("tm", "obs", None)),
        check_vma=False,
    )
```

profile of v0, /device:TPU:0, one launch (start us, length us, event | category | flops | bytes accessed | tf_op | source)
XLA Modules:
  0.0 207.5 jit_solution(11546981965205448874)
XLA Ops:
  7.2 0.7 fusion.8
  8.0 0.8 select_reduce_fusion.3
  9.5 0.8 select_reduce_fusion.2
  11.0 0.8 scatter_custom_fusion.1
  11.8 0.7 all_to_all.22
  12.5 7.4 %all-to-all-start.1 = ((s32[16,1,8]{2,1,0:T(1,128)}), s32[16,1,8]{2,1,0:T(1,128)S(1)}, u32[]{:S(2)}, u32[]{:S(2)}) async-start(s32[16,1,8]{2,1,0:T(1,128)} %bitcast.8), calls=%async_computation.1 | async-start | bytes 16384 | tf_op jit(solution)/shard_map/all_to_all | solution.py:43
  19.9 7.0 %scatter_custom_fusion = bf16[128,16384]{1,0:T(8,128)(2,1)} fusion(s32[64]{0:T(128)S(1)} %fusion.10, bf16[64,16384]{1,0:T(8,128)(2,1)} %param.10, bf16[]{:T(256)} %constant.7.clone.1), kind=kCustom, calls=%fused_computation.12 | custom fusion | bytes 4194816 | tf_op jit(solution)/shard_map/scatter | solution.py:35
  26.9 6.2 %all-to-all-start = ((bf16[16,8,16384]{2,1,0:T(8,128)(2,1)}), bf16[16,8,16384]{2,1,0:T(8,128)(2,1)}, u32[]{:S(2)}, u32[]{:S(2)}) async-start(bf16[16,8,16384]{2,1,0:T(8,128)(2,1)} %bitcast.37), calls=%async_computation | async-start | bytes 8388608 | tf_op jit(solution)/shard_map/all_to_all | solution.py:42
  33.1 9.2 %all_gather.3 = bf16[4,4,16384]{2,1,0:T(4,128)(2,1)S(1)} all-gather(bf16[2,4,16384]{2,1,0:T(4,128)(2,1)S(1)} %copy-done), channel_id=1, replica_groups=mesh['tm'=2,'obs'=16] {'tm'}, dimensions={0}, use_global_device_ids=true | all-gather | bytes 786432 | tf_op jit(solution)/shard_map/all_gather | solution.py:40
  43.8 5.2 %gather_fusion = bf16[128,16384]{1,0:T(8,128)(2,1)} fusion(bf16[16,16384]{1,0:T(8,128)(2,1)S(1)} %reshape.77, s32[1024]{0:T(1024)S(1)} %pad_clamp_fusion.1), kind=kCustom, calls=%fused_computation | custom fusion | bytes 8389120 | tf_op jit(solution)/shard_map/gather | solution.py:45
  48.9 61.7 %all-to-all-done = bf16[16,8,16384]{2,1,0:T(8,128)(2,1)} async-done(((bf16[16,8,16384]{2,1,0:T(8,128)(2,1)}), bf16[16,8,16384]{2,1,0:T(8,128)(2,1)}, u32[]{:S(2)}, u32[]{:S(2)}) %all-to-all-start) | async-done | bytes 4194336 | tf_op jit(solution)/shard_map/all_to_all | solution.py:42
  110.6 5.3 %fusion = f32[16,8]{1,0:T(8,128)} fusion(bf16[16,8,16384]{2,1,0:T(8,128)(2,1)} %all-to-all-done, bf16[128,16384]{1,0:T(8,128)(2,1)} %gather_fusion), kind=kLoop, calls=%fused_computation.7 | loop fusion | flops 8388480 | bytes 8389120
  115.9 19.6 %all-to-all-start.2 = ((f32[16,1,8]{2,1,0:T(1,128)}), f32[16,1,8]{2,1,0:T(1,128)S(1)}, u32[]{:S(2)}, u32[]{:S(2)}) async-start(f32[16,1,8]{2,1,0:T(1,128)} %bitcast.17), calls=%async_computation.2 | async-start | bytes 16384 | tf_op jit(solution)/shard_map/all_to_all | solution.py:46
  135.6 6.3 %all-to-all-done.2 = f32[16,1,8]{2,1,0:T(1,128)S(1)} async-done(((f32[16,1,8]{2,1,0:T(1,128)}), f32[16,1,8]{2,1,0:T(1,128)S(1)}, u32[]{:S(2)}, u32[]{:S(2)}) %all-to-all-start.2) | async-done | bytes 544 | tf_op jit(solution)/shard_map/all_to_all | solution.py:46
  143.2 0.8 gather_fusion.1
  144.3 0.8 scatter_custom_fusion.2
  145.1 0.7 all_to_all.26
  145.8 3.5 %all-to-all-start.3 = ((f32[16,1,8]{2,1,0:T(1,128)}), f32[16,1,8]{2,1,0:T(1,128)S(1)}, u32[]{:S(2)}, u32[]{:S(2)}) async-start(f32[16,1,8]{2,1,0:T(1,128)} %bitcast.14), calls=%async_computation.3 | async-start | bytes 16384 | tf_op jit(solution)/shard_map/all_to_all | solution.py:58
  149.6 6.0 %all-to-all-done.3 = f32[16,1,8]{2,1,0:T(1,128)S(1)} async-done(((f32[16,1,8]{2,1,0:T(1,128)}), f32[16,1,8]{2,1,0:T(1,128)S(1)}, u32[]{:S(2)}, u32[]{:S(2)}) %all-to-all-start.3) | async-done | bytes 544 | tf_op jit(solution)/shard_map/all_to_all | solution.py:58
  155.6 3.1 %fusion.3 = f32[16,16384]{1,0:T(8,128)S(1)} fusion(bf16[16,8,16384]{2,1,0:T(8,128)(2,1)} %all-to-all-done, f32[16,8]{1,0:T(8,128)S(1)} %bitcast.39, s32[128]{0:T(128)S(1)} %eq.54), kind=kOutput, calls=%fused_computation.10 | convolution fusion | flops 73402368 | bytes 5243904 | tf_op jit(solution)/shard_map/dot_general | solution.py:68
  158.6 1.7 reshape.82
  161.6 36.3 %all-reduce.3.cloned.1.call-done = f32[4,65536]{1,0:T(4,128)} async-done(((f32[4,65536]{1,0:T(4,128)}), f32[4,65536]{1,0:T(4,128)}) %all-reduce.3.cloned.1.call-update) | async-done | bytes 1048592
  197.9 1.4 constant_dynamic-slice_fusion
  199.3 1.3 reshape.83
  (33 shorter events, 5.3 us)
Async XLA Ops:
  12.5 14.4 %all-to-all-start.1 = ((s32[16,1,8]{2,1,0:T(1,128)}), s32[16,1,8]{2,1,0:T(1,128)S(1)}, u32[]{:S(2)}, u32[]{:S(2)}) async-start(s32[16,1,8]{2,1,0:T(1,128)} %bitcast.8), calls=%async_computation.1 | async-start | bytes 16384 | tf_op jit(solution)/shard_map/all_to_all | solution.py:43
  26.9 6.2 %copy-start = (bf16[2,4,16384]{2,1,0:T(4,128)(2,1)S(1)}, bf16[2,4,16384]{2,1,0:T(4,128)(2,1)}, u32[]{:S(2)}) copy-start(bf16[2,4,16384]{2,1,0:T(4,128)(2,1)} %param.9) | copy-start | bytes 786436
  26.9 83.7 %all-to-all-start = ((bf16[16,8,16384]{2,1,0:T(8,128)(2,1)}), bf16[16,8,16384]{2,1,0:T(8,128)(2,1)}, u32[]{:S(2)}, u32[]{:S(2)}) async-start(bf16[16,8,16384]{2,1,0:T(8,128)(2,1)} %bitcast.37), calls=%async_computation | async-start | bytes 8388608 | tf_op jit(solution)/shard_map/all_to_all | solution.py:42
  48.9 95.0 %copy-start.4 = (s32[1,64]{1,0:T(1,128)S(1)}, s32[1,64]{1,0:T(1,128)}, u32[]{:S(2)}) copy-start(s32[1,64]{1,0:T(1,128)} %param.14) | copy-start | bytes 772
  48.9 95.2 %copy-start.1 = (f32[1,16]{1,0:T(1,128)S(1)}, f32[1,16]{1,0:T(1,128)}, u32[]{:S(2)}) copy-start(f32[1,16]{1,0:T(1,128)} %param.17) | copy-start | bytes 196
  48.9 95.2 %copy-start.2 = (f32[1,16]{1,0:T(1,128)S(1)}, f32[1,16]{1,0:T(1,128)}, u32[]{:S(2)}) copy-start(f32[1,16]{1,0:T(1,128)} %param.16) | copy-start | bytes 196
  115.9 26.0 %all-to-all-start.2 = ((f32[16,1,8]{2,1,0:T(1,128)}), f32[16,1,8]{2,1,0:T(1,128)S(1)}, u32[]{:S(2)}, u32[]{:S(2)}) async-start(f32[16,1,8]{2,1,0:T(1,128)} %bitcast.17), calls=%async_computation.2 | async-start | bytes 16384 | tf_op jit(solution)/shard_map/all_to_all | solution.py:46
  144.1 16.3 %copy-start.3 = (f32[16]{0:T(128)}, f32[16]{0:T(128)S(1)}, u32[]{:S(2)}) copy-start(f32[16]{0:T(128)S(1)} %select_reduce_fusion.1) | copy-start | bytes 196
  145.8 9.8 %all-to-all-start.3 = ((f32[16,1,8]{2,1,0:T(1,128)}), f32[16,1,8]{2,1,0:T(1,128)S(1)}, u32[]{:S(2)}, u32[]{:S(2)}) async-start(f32[16,1,8]{2,1,0:T(1,128)} %bitcast.14), calls=%async_computation.3 | async-start | bytes 16384 | tf_op jit(solution)/shard_map/all_to_all | solution.py:58
  149.2 48.6 %all-reduce.3.cloned.1.call-start = ((), (), s32[]{:S(2)}) async-start(), calls=%async_computation.4 | async-start | bytes 2097152
  155.6 4.8 %copy-start.5 = (u32[32]{0:T(128)S(1)}, u32[32]{0:T(128)}, u32[]{:S(2)}) copy-start(u32[32]{0:T(128)} %constant.31) | copy-start | bytes 388
Sparse Core Ops, SparseCore 0:
  160.5 37.3 all-reduce.2
where the time goes:
time: 208 us
  waiting for transfers between devices  110 us (53%)
  starting transfers between devices  36.9 us (18%)
  local copies, waits for them, and re-layouts  22.3 us (11%)
  between operations  14.9 us (7%)
  other arithmetic  10.8 us (5%)
  blocking collectives  9.23 us (4%)
  matrix products  3.08 us (1%)
    all_to_all x1, waiting for transfers between devices, per_device(): lax.all_to_all(send_blocks, 'obs', split_axis=0, concat_axis=0, tiled=True)  61.7 us
    unnamed x2, waiting for transfers between devices  36.3 us
    all_to_all x1, starting transfers between devices, per_device(): lax.all_to_all(jnp.einsum('pkc,pkc->pk', got_blocks, selected, preferred_...  19.6 us
    all_gather x1, blocking collectives, per_device(): lax.all_gather(flux, 'tm', axis=0, tiled=True).reshape(-1, cell_count)  9.23 us
    all_to_all x1, starting transfers between devices, per_device(): lax.all_to_all(send_target, 'obs', split_axis=0, concat_axis=0, tiled=True)  7.39 us
    scatter x1, local copies, waits for them, and re-layouts, per_device(): jnp.zeros((peer_count * slot_cap, cell_count), jnp.bfloat16).at[slot_index]  6.98 us
    all_to_all x1, waiting for transfers between devices, per_device(): lax.all_to_all(jnp.einsum('pkc,pkc->pk', got_blocks, selected, preferred_...  6.35 us
    all_to_all x1, starting transfers between devices, per_device(): lax.all_to_all(send_blocks, 'obs', split_axis=0, concat_axis=0, tiled=True)  6.19 us
  transfers between devices with their start and end apart: 5, of which 4 were waited for; matrix products, arithmetic and copies ran while one was open for 7% of the time, Pallas kernels for 0%

commit v1 on v0

--- a/solution.py
+++ b/solution.py
@@ -1,6 +1,10 @@
+import functools
+
 import jax
 import jax.numpy as jnp
 from jax import lax
+from jax.experimental import pallas as pl
+from jax.experimental.pallas import tpu as pltpu
 from jax.sharding import PartitionSpec as P
 
 
@@ -73,6 +77,406 @@
     return (modeled[None, :], gradient)
 
 
+KINDS = (
+    "foot", "flux", "m0", "m1", "m2", "m3", "m4", "m5", "m6", "vals",
+    "gup", "gdown", "g1x", "g1y", "g2x", "g2y",
+    "s1x", "s1y", "s2x", "s2y", "up0", "up1", "down0", "down1", "fin",
+)
+KIND = {name: at for at, name in enumerate(KINDS)}
+
+
+def eye(n):
+    return lax.broadcasted_iota(jnp.int32, (n, n), 0) == lax.broadcasted_iota(jnp.int32, (n, n), 1)
+
+
+def to_col(row):
+    return jnp.sum(jnp.where(eye(row.shape[1]), row, 0.0), axis=1, keepdims=True)
+
+
+def to_row(col):
+    return jnp.sum(jnp.where(eye(col.shape[0]), col, 0.0), axis=0, keepdims=True)
+
+
+def chip_kernel(
+    depth, windows, tile_dev, flux, foot, owner, tile, lag, sounding, swin, observed, weight,
+    modeled_out, out,
+    foot_all, contrib, gath, owner_p, tile_p, lag_p, sounding_p, swin_p, observed_p, weight_p,
+    val_send, val_recv, row_ids, t1x, t1y, a1x, a1y, t2x, t2y, a2x, a2y, zsum, zup, zdown,
+    send_sem, recv_sem, local_sem,
+):
+    entries = foot.shape[0]
+    half = foot.shape[1] // 2
+    quarter = half // 2
+    rows_dev = flux.shape[0]
+    rows_chip = 2 * rows_dev
+    rows_plane = 4 * rows_chip
+    tile_cells = min(1024, quarter)
+    tile_back = min(512, quarter)
+    y = lax.axis_index("tm")
+    o = lax.axis_index("obs")
+    core = lax.rem(o, 2)
+    x = lax.rem(o // 2, 2)
+    z = o // 4
+    partner = (y, o + 1 - 2 * core)
+    xn = (y, o + 2 - 4 * x)
+    yn = (1 - y, o)
+    zu = (y, o + 4)
+    zd = (y, o - 4)
+    has_up = z < depth - 1
+    has_down = z > 0
+
+    def signal(device):
+        pl.semaphore_signal(
+            barrier, inc=1, device_id=device, device_id_type=pl.DeviceIdType.MESH
+        )
+
+    barrier = pltpu.get_barrier_semaphore()
+    for device in (partner, xn, yn):
+        signal(device)
+    pl.when(has_up)(lambda: signal(zu))
+    pl.when(has_down)(lambda: signal(zd))
+    peers = 3 + jnp.where(has_up, 1, 0) + jnp.where(has_down, 1, 0)
+    pl.semaphore_wait(barrier, peers)
+
+    def remote(kind, at, src, dst, device):
+        return pltpu.make_async_remote_copy(
+            src_ref=src,
+            dst_ref=dst,
+            send_sem=send_sem.at[KIND[kind], at],
+            recv_sem=recv_sem.at[KIND[kind], at],
+            device_id=device,
+            device_id_type=pl.DeviceIdType.MESH,
+        )
+
+    mine = pl.ds(pl.multiple_of(core * half, half), half)
+    other = pl.ds(pl.multiple_of((1 - core) * half, half), half)
+    my_rows = pl.ds(pl.multiple_of(core * rows_dev, rows_dev), rows_dev)
+    low, high = pl.ds(0, quarter), pl.ds(quarter, quarter)
+
+    fixed = [
+        remote("flux", 0, flux.at[:, other], gath.at[z, y, x, my_rows, :], partner),
+        remote("foot", 0, foot.at[:, other], foot_all.at[1], partner),
+    ]
+    pairs = (
+        (owner, owner_p), (tile, tile_p), (lag, lag_p), (sounding, sounding_p),
+        (swin, swin_p), (observed, observed_p), (weight, weight_p),
+    )
+    for at, (src, dst) in enumerate(pairs):
+        fixed.append(remote(f"m{at}", 0, src, dst, partner))
+    local_flux = pltpu.make_async_copy(flux.at[:, mine], gath.at[z, y, x, my_rows, :], local_sem.at[0])
+    local_foot = pltpu.make_async_copy(foot.at[:, mine], foot_all.at[0], local_sem.at[1])
+    local_flux.start()
+    for copy in fixed:
+        copy.start()
+    local_foot.start()
+
+    def nearest(k):
+        picked = z
+        for place in range(depth):
+            order = sorted(range(depth), key=lambda other_z: (abs(other_z - place), other_z))
+            picked = jnp.where(z == place, order[k], picked)
+        return picked
+
+    def gather_z(zz, upward):
+        block = gath.at[zz, y, x]
+        return remote("gup" if upward else "gdown", zz, block, block, zu if upward else zd)
+
+    def gather_1x(zz):
+        block = gath.at[zz, y, x, :, low]
+        return remote("g1x", zz, block, block, xn)
+
+    def gather_1y(zz):
+        block = gath.at[zz, y, x, :, high]
+        return remote("g1y", zz, block, block, yn)
+
+    def gather_2x(zz):
+        block = gath.at[zz, :, x, :, high]
+        return remote("g2x", zz, block, block, xn)
+
+    def gather_2y(zz):
+        block = gath.at[zz, y, :, :, low]
+        return remote("g2y", zz, block, block, yn)
+
+    def fields(refs):
+        owner_r, tile_r, lag_r, sounding_r, swin_r, _, _ = refs
+        count = swin_r.shape[1]
+        hot = lax.broadcasted_iota(jnp.int32, (count, entries), 0) == sounding_r[...]
+        window = jnp.sum(
+            jnp.where(hot, to_col(swin_r[...].astype(jnp.float32)), 0.0), axis=0, keepdims=True
+        ) - lag_r[...].astype(jnp.float32)
+        window = window.astype(jnp.int32)
+        own = to_row(owner_r[...].astype(jnp.float32)).astype(jnp.int32)
+        late = jnp.where(window >= windows, 1, 0)
+        chip = ((own >> 2) * 2 + late) * 2 + ((own >> 1) & 1)
+        inner = (own & 1) * rows_dev + (window - late * windows) * tile_dev + tile_r[...]
+        return hot, chip * rows_chip + inner
+
+    sets = (
+        (owner, tile, lag, sounding, swin, observed, weight),
+        (owner_p, tile_p, lag_p, sounding_p, swin_p, observed_p, weight_p),
+    )
+    hots, ids = [None, None], [None, None]
+    hots[0], ids[0] = fields(sets[0])
+
+    local_flux.wait()
+    fixed[0].wait_recv()
+    total = [jnp.zeros((entries, 1), jnp.float32)] * 2
+    id_cols = [None, None]
+    for k in range(depth + 2):
+        if k < depth:
+            zz = nearest(k)
+            if k > 0:
+                pl.when(zz < z)(lambda: gather_z(zz, True).wait_recv())
+                pl.when(zz > z)(lambda: gather_z(zz, False).wait_recv())
+            pl.when((zz <= z) & has_up)(lambda: gather_z(zz, True).start())
+            pl.when((zz >= z) & has_down)(lambda: gather_z(zz, False).start())
+            gather_1x(zz).start()
+            gather_1y(zz).start()
+        if k == 1:
+            for copy in fixed[1:]:
+                copy.wait_recv()
+            local_foot.wait()
+            hots[1], ids[1] = fields(sets[1])
+            id_cols = [to_col(i.astype(jnp.float32)).astype(jnp.int32) for i in ids]
+            row_ids[...] = jnp.concatenate(ids, axis=1)
+        if 1 <= k <= depth:
+            zz = nearest(k - 1)
+            gather_1x(zz).wait_recv()
+            gather_1y(zz).wait_recv()
+            gather_2x(zz).start()
+            gather_2y(zz).start()
+        if k >= 2:
+            zz = nearest(k - 2)
+            gather_2x(zz).wait_recv()
+            gather_2y(zz).wait_recv()
+
+            def dots(step, acc):
+                cells = pl.ds(pl.multiple_of(step * tile_cells, tile_cells), tile_cells)
+                block = gath[zz, :, :, :, cells].reshape(rows_plane, tile_cells)
+                return tuple(
+                    acc[h]
+                    + lax.dot_general(
+                        foot_all[h, :, cells], block, (((1,), (1,)), ((), ())),
+                        preferred_element_type=jnp.float32,
+                    )
+                    for h in range(2)
+                )
+
+            zero = jnp.zeros((entries, rows_plane), jnp.float32)
+            acc = lax.fori_loop(0, half // tile_cells, dots, (zero, zero))
+            lanes = lax.broadcasted_iota(jnp.int32, (entries, rows_plane), 1) + zz * rows_plane
+            for h in range(2):
+                total[h] = total[h] + jnp.sum(
+                    jnp.where(id_cols[h] == lanes, acc[h], 0.0), axis=1, keepdims=True
+                )
+
+    for h in range(2):
+        val_send[h] = to_row(total[h])
+    vals = remote("vals", 0, val_send, val_recv, partner)
+    vals.start()
+    vals.wait_recv()
+    for h in range(2):
+        value = val_send[h] + val_recv[1 - h]
+        modeled = to_row(jnp.sum(jnp.where(hots[h], value, 0.0), axis=1, keepdims=True))
+        if h == 0:
+            modeled_out[...] = modeled
+        residual = sets[h][6][...] * (modeled - sets[h][5][...])
+        resid = to_col(
+            jnp.sum(jnp.where(hots[h], to_col(residual), 0.0), axis=0, keepdims=True)
+        )
+
+        def scale(step, carry):
+            cells = pl.ds(pl.multiple_of(step * tile_cells, tile_cells), tile_cells)
+            scaled = resid * foot_all[h, :, cells].astype(jnp.float32)
+            contrib[pl.ds(h * entries, entries), cells] = scaled.astype(jnp.bfloat16)
+            return carry
+
+        lax.fori_loop(0, half // tile_cells, scale, 0)
+
+    def partial(rows, cells):
+        pick = jnp.where(row_ids[...] == rows, 1.0, 0.0).astype(jnp.bfloat16)
+        return jnp.dot(pick, contrib[:, cells], preferred_element_type=jnp.float32)
+
+    def over(offset, body):
+        def step_body(step, carry):
+            at = pl.multiple_of(step * tile_back, tile_back)
+            body(pl.ds(at, tile_back), pl.ds(offset + at, tile_back))
+            return carry
+
+        lax.fori_loop(0, quarter // tile_back, step_body, 0)
+
+    def rows_of(zz, yy, xx):
+        base = ((zz * 2 + yy) * 2 + xx) * rows_chip
+        return lax.broadcasted_iota(jnp.int32, (rows_chip, 2 * entries), 0) + base
+
+    def scatter_1x(zz):
+        return remote("s1x", zz, t1x.at[zz], a1x.at[zz], xn)
+
+    def scatter_1y(zz):
+        return remote("s1y", zz, t1y.at[zz], a1y.at[zz], yn)
+
+    def scatter_2x(zz):
+        return remote("s2x", zz, t2x.at[zz], a2x.at[zz], xn)
+
+    def scatter_2y(zz):
+        return remote("s2y", zz, t2y.at[zz], a2y.at[zz], yn)
+
+    def scatter_z(zz, part, upward):
+        cells = high if part else low
+        kind = ("up" if upward else "down") + str(part)
+        into = zup if upward else zdown
+        return remote(kind, zz, zsum.at[zz, :, :, cells], into.at[zz, :, :, cells], zu if upward else zd)
+
+    def finish(part, far):
+        cells = high if part else low
+        into = pl.ds(pl.multiple_of(core * half + part * quarter, quarter), quarter)
+        if far:
+            return remote("fin", part, zsum.at[z, 1 - core, :, cells], out.at[:, into], partner)
+        return pltpu.make_async_copy(zsum.at[z, core, :, cells], out.at[:, into], local_sem.at[part])
+
+    def first(zz):
+        row_x = jnp.concatenate([rows_of(zz, 0, 1 - x), rows_of(zz, 1, 1 - x)], axis=0)
+        row_y = jnp.concatenate([rows_of(zz, 1 - y, 0), rows_of(zz, 1 - y, 1)], axis=0)
+
+        def for_x(near, cells):
+            t1x[zz, :, :, near] = (
+                partial(row_x, cells).astype(jnp.bfloat16).reshape(2, rows_chip, tile_back)
+            )
+
+        def for_y(near, cells):
+            t1y[zz, :, :, near] = (
+                partial(row_y, cells).astype(jnp.bfloat16).reshape(2, rows_chip, tile_back)
+            )
+
+        over(0, for_x)
+        scatter_1x(zz).start()
+        over(quarter, for_y)
+        scatter_1y(zz).start()
+
+    def second(zz):
+        def for_y(near, cells):
+            got = a1x[zz, 1 - y, :, near].astype(jnp.float32)
+            t2y[zz, :, near] = (partial(rows_of(zz, 1 - y, x), cells) + got).astype(jnp.bfloat16)
+
+        def for_x(near, cells):
+            got = a1y[zz, 1 - x, :, near].astype(jnp.float32)
+            t2x[zz, :, near] = (partial(rows_of(zz, y, 1 - x), cells) + got).astype(jnp.bfloat16)
+
+        scatter_1x(zz).wait_recv()
+        over(0, for_y)
+        scatter_2y(zz).start()
+        scatter_1y(zz).wait_recv()
+        over(quarter, for_x)
+        scatter_2x(zz).start()
+
+    def third(zz, part):
+        def gather_sum(near, cells):
+            if part:
+                got = a1y[zz, x, :, near].astype(jnp.float32) + a2x[zz, :, near].astype(jnp.float32)
+            else:
+                got = a1x[zz, y, :, near].astype(jnp.float32) + a2y[zz, :, near].astype(jnp.float32)
+            summed = partial(rows_of(zz, y, x), cells) + got
+            zsum[zz, :, :, cells] = summed.reshape(2, rows_dev, tile_back)
+
+        def add_from(source):
+            def body(near, cells):
+                zsum[zz, :, :, cells] = zsum[zz, :, :, cells] + source[zz, :, :, cells]
+
+            return body
+
+        (scatter_2x if part else scatter_2y)(zz).wait_recv()
+        over(part * quarter, gather_sum)
+
+        @pl.when((zz >= z) & has_down)
+        def _():
+            scatter_z(zz, part, True).wait_recv()
+            over(part * quarter, add_from(zup))
+
+        @pl.when((zz <= z) & has_up)
+        def _():
+            scatter_z(zz, part, False).wait_recv()
+            over(part * quarter, add_from(zdown))
+
+        pl.when(zz > z)(lambda: scatter_z(zz, part, True).start())
+        pl.when(zz < z)(lambda: scatter_z(zz, part, False).start())
+
+    for k in range(depth + 2):
+        if k < depth:
+            first(nearest(depth - 1 - k))
+        if 1 <= k <= depth:
+            second(nearest(depth - k))
+        if k >= 2:
+            for part in range(2):
+                third(nearest(depth + 1 - k), part)
+                if k == depth + 1:
+                    finish(part, True).start()
+                    finish(part, False).start()
+    for part in range(2):
+        finish(part, False).wait()
+        finish(part, True).wait()
+    for copy in fixed:
+        copy.wait_send()
+    vals.wait_send()
+
+    def drain(zz, carry):
+        pl.when((zz <= z) & has_up)(lambda: gather_z(zz, True).wait_send())
+        pl.when((zz >= z) & has_down)(lambda: gather_z(zz, False).wait_send())
+        for copy in (
+            gather_1x, gather_1y, gather_2x, gather_2y,
+            scatter_1x, scatter_1y, scatter_2x, scatter_2y,
+        ):
+            copy(zz).wait_send()
+        for part in range(2):
+            pl.when(zz > z)(lambda: scatter_z(zz, part, True).wait_send())
+            pl.when(zz < z)(lambda: scatter_z(zz, part, False).wait_send())
+        return carry
+
+    lax.fori_loop(0, depth, drain, 0)
+
+
+def per_chip(depth, flux, footprint, owner, tile, lag, sounding, swin, observed, weight):
+    windows, tile_dev, cells = flux.shape
+    entries = footprint.shape[0]
+    rows_dev = windows * tile_dev
+    rows_chip = 2 * rows_dev
+    half, quarter = cells // 2, cells // 4
+    sounds = observed.shape[1]
+    bf, f32, i32 = jnp.bfloat16, jnp.float32, jnp.int32
+    vmem, hbm = pl.BlockSpec(memory_space=pltpu.VMEM), pl.BlockSpec(memory_space=pl.ANY)
+    modeled, gradient = pl.pallas_call(
+        functools.partial(chip_kernel, depth, windows, tile_dev),
+        out_shape=(
+            jax.ShapeDtypeStruct((1, sounds), f32),
+            jax.ShapeDtypeStruct((rows_dev, cells), f32),
+        ),
+        in_specs=[hbm, hbm] + [vmem] * 7,
+        out_specs=(vmem, vmem),
+        scratch_shapes=[
+            pltpu.VMEM((2, entries, half), bf),
+            pltpu.VMEM((2 * entries, half), bf),
+            pltpu.VMEM((depth, 2, 2, rows_chip, half), bf),
+            pltpu.VMEM((entries, 1), i32),
+            pltpu.VMEM((1, entries), i32),
+            pltpu.VMEM((1, entries), i32),
+            pltpu.VMEM((1, entries), i32),
+            pltpu.VMEM((1, sounds), i32),
+            pltpu.VMEM((1, sounds), f32),
+            pltpu.VMEM((1, sounds), f32),
+            pltpu.VMEM((2, 1, entries), f32),
+            pltpu.VMEM((2, 1, entries), f32),
+            pltpu.VMEM((1, 2 * entries), i32),
+            *[pltpu.VMEM((depth, 2, rows_chip, quarter), bf)] * 4,
+            *[pltpu.VMEM((depth, rows_chip, quarter), bf)] * 4,
+            *[pltpu.VMEM((depth, 2, rows_dev, half), f32)] * 3,
+            pltpu.SemaphoreType.DMA((len(KINDS), depth)),
+            pltpu.SemaphoreType.DMA((len(KINDS), depth)),
+            pltpu.SemaphoreType.DMA((2,)),
+        ],
+        compiler_params=pltpu.CompilerParams(collective_id=0, has_side_effects=True),
+    )(flux.reshape(rows_dev, cells), footprint, owner, tile, lag, sounding, swin, observed, weight)
+    return modeled, gradient.reshape(windows, tile_dev, cells)
+
+
 def solution(mesh):
     placed = (
         P("tm", "obs", None),
@@ -85,8 +489,19 @@
         P(("tm", "obs"), None),
         P(("tm", "obs"), None),
     )
+    times, places = mesh.shape["tm"], mesh.shape["obs"]
+    depth = places // 4
+    grouped = times == 2 and places % 4 == 0 and depth >= 2
+
+    def routed(flux, *rest):
+        rows = flux.shape[0] * flux.shape[1] * times * places
+        fits = rows * flux.shape[2] * 8 <= 40 * 2**20
+        plain = flux.shape[0] * flux.shape[1] % 8 == 0 and flux.shape[2] % 2048 == 0
+        body = functools.partial(per_chip, depth) if grouped and fits and plain else per_device
+        return body(flux, *rest)
+
     return jax.shard_map(
-        per_device,
+        routed,
         mesh=mesh,
         in_specs=placed,
         out_specs=(P(("tm", "obs"), None), P("tm", "obs", None)),

time: 208 us -> 122 us (0.59)
  Pallas kernels: 0 us -> 115 us
  waiting for transfers between devices: 110 us -> 0 us
  starting transfers between devices: 36.9 us -> 0 us
  local copies, waits for them, and re-layouts: 22.3 us -> 6.2 us
  between operations: 14.9 us -> 0.64 us
  other arithmetic: 10.8 us -> 0 us
  blocking collectives: 9.23 us -> 0 us
  matrix products: 3.08 us -> 0 us
    pallas_call x0 -> x1, Pallas kernels: none -> 115 us  [per_chip(): pl.pallas_call(functools.partial(chip_kernel, depth, windows, tile_dev),...]
    all_to_all x4 -> x0, waiting for transfers between devices: 74.1 us -> none  [the longest x1 61.7 us: per_device(): lax.all_to_all(send_blocks, 'obs', split_axis=0, concat_axis=0, tiled=True)]
    all_to_all x4 -> x0, starting transfers between devices: 36.7 us -> none  [the longest x1 19.6 us: per_device(): lax.all_to_all(jnp.einsum('pkc,pkc->pk', got_blocks, selected, preferred_...]
    unnamed x2 -> x0, waiting for transfers between devices: 36.3 us -> none
    all_gather x1 -> x0, blocking collectives: 9.23 us -> none  [per_device(): lax.all_gather(flux, 'tm', axis=0, tiled=True).reshape(-1, cell_count)]
    scatter x3 -> x0, local copies, waits for them, and re-layouts: 8.54 us -> none  [the longest x1 6.98 us: per_device(): jnp.zeros((peer_count * slot_cap, cell_count), jnp.bfloat16).at[slot_index]]
    gather x2 -> x0, local copies, waits for them, and re-layouts: 5.94 us -> none  [the longest x1 5.16 us: per_device(): selected = everything[got_target.reshape(-1)].reshape(got_blocks.shape)]
    unnamed x1 -> x0, other arithmetic: 5.27 us -> none
  transfers between devices with their start and end apart: 5 -> 0, of which waited for: 4 -> 0; matrix products, arithmetic and copies ran while one was open for 7% -> 0% of each run, Pallas kernels for 0% -> 0%
where the time goes in v1:
time: 122 us
  Pallas kernels  115 us (94%)
  local copies, waits for them, and re-layouts  6.2 us (5%)
    pallas_call x1, Pallas kernels, per_chip(): pl.pallas_call(functools.partial(chip_kernel, depth, windows, tile_dev),...  115 us
    unnamed x2, local copies, waits for them, and re-layouts  2.5 us

profile of v1, /device:TPU:0, one launch (start us, length us, event | category | flops | bytes accessed | tf_op | source)
XLA Modules:
  0.0 121.9 jit_solution(10259762418967079678)
XLA Ops:
  0.6 1.4 %copy.11.owner = s32[64,1]{1,0:T(8,128)} copy(s32[64,1]{0,1:T(1,128)} %param.11) | data formatting | bytes 512 | tf_op args[2]
  2.0 1.7 %reshape.10.flux = bf16[8,16384]{1,0:T(8,128)(2,1)} reshape(bf16[2,4,16384]{2,1,0:T(4,128)(2,1)} %param.9) | data formatting | bytes 524288 | tf_op jit(solution)/shard_map/reshape | solution.py:476
  3.7 115.1 %shard_map.104 = (f32[1,16]{1,0:T(1,128)}, f32[8,16384]{1,0:T(8,128)}) custom-call(bf16[8,16384]{1,0:T(8,128)(2,1)} %reshape.10.flux, bf16[64,16384]{1,0:T(8,128)(2,1)} %foot.1, s32[64,1]{1,0:T(8,128)} %copy.11.owner, s32[1,64]{1,0:T(1,128)} %tile.1, s32[1,64]{1,0:T(1,128)} %lag.1, s32[1,64]{1,0:T(1,128)} %sounding.1, s32[1,16]{1,0:T(1,128)} %swin.1, ...), custom_call_target="tpu_custom_call" | custom-call | tf_op jit(solution)/shard_map/pallas_call | solution.py:446
  118.8 2.0 %reshape.11 = f32[2,4,16384]{2,1,0:T(4,128)} reshape(f32[8,16384]{1,0:T(8,128)} %get-tuple-element.5) | data formatting | bytes 1048576 | tf_op jit(solution)/shard_map/reshape | solution.py:477
  120.8 1.1 copy.13

commit v2 on v1

--- a/solution.py
+++ b/solution.py
@@ -80,7 +80,7 @@
 KINDS = (
     "foot", "flux", "m0", "m1", "m2", "m3", "m4", "m5", "m6", "vals",
     "gup", "gdown", "g1x", "g1y", "g2x", "g2y",
-    "s1x", "s1y", "s2x", "s2y", "up0", "up1", "down0", "down1", "fin",
+    "s1x", "s1y", "s2x", "s2y", "z0", "z1", "fin",
 )
 KIND = {name: at for at, name in enumerate(KINDS)}
 
@@ -101,17 +101,17 @@
     depth, windows, tile_dev, flux, foot, owner, tile, lag, sounding, swin, observed, weight,
     modeled_out, out,
     foot_all, contrib, gath, owner_p, tile_p, lag_p, sounding_p, swin_p, observed_p, weight_p,
-    val_send, val_recv, row_ids, t1x, t1y, a1x, a1y, t2x, t2y, a2x, a2y, zsum, zup, zdown,
+    val_send, val_recv, row_ids, staged, t1x, t1y, a1x, a1y, t2x, t2y, a2x, a2y, keep_x, keep_y, tz, az, zsum,
     send_sem, recv_sem, local_sem,
 ):
     entries = foot.shape[0]
     half = foot.shape[1] // 2
     quarter = half // 2
-    rows_dev = flux.shape[0]
+    rows_dev = windows * tile_dev
     rows_chip = 2 * rows_dev
     rows_plane = 4 * rows_chip
     tile_cells = min(1024, quarter)
-    tile_back = min(512, quarter)
+    tile_back = min(1024, quarter)
     y = lax.axis_index("tm")
     o = lax.axis_index("obs")
     core = lax.rem(o, 2)
@@ -125,18 +125,22 @@
     has_up = z < depth - 1
     has_down = z > 0
 
-    def signal(device):
+    def nearest(k):
+        picked = z
+        for place in range(depth):
+            order = sorted(range(depth), key=lambda other_z: (abs(other_z - place), other_z))
+            picked = jnp.where(z == place, order[k], picked)
+        return picked
+
+    def along_z(zz):
+        return (y, o + 4 * (zz - z))
+
+    barrier = pltpu.get_barrier_semaphore()
+    for device in (partner, xn, yn, *(along_z(nearest(k)) for k in range(1, depth))):
         pl.semaphore_signal(
             barrier, inc=1, device_id=device, device_id_type=pl.DeviceIdType.MESH
         )
-
-    barrier = pltpu.get_barrier_semaphore()
-    for device in (partner, xn, yn):
-        signal(device)
-    pl.when(has_up)(lambda: signal(zu))
-    pl.when(has_down)(lambda: signal(zd))
-    peers = 3 + jnp.where(has_up, 1, 0) + jnp.where(has_down, 1, 0)
-    pl.semaphore_wait(barrier, peers)
+    pl.semaphore_wait(barrier, 2 + depth)
 
     def remote(kind, at, src, dst, device):
         return pltpu.make_async_remote_copy(
@@ -150,11 +154,10 @@
 
     mine = pl.ds(pl.multiple_of(core * half, half), half)
     other = pl.ds(pl.multiple_of((1 - core) * half, half), half)
-    my_rows = pl.ds(pl.multiple_of(core * rows_dev, rows_dev), rows_dev)
     low, high = pl.ds(0, quarter), pl.ds(quarter, quarter)
 
     fixed = [
-        remote("flux", 0, flux.at[:, other], gath.at[z, y, x, my_rows, :], partner),
+        remote("flux", 0, flux.at[:, :, other], staged.at[1], partner),
         remote("foot", 0, foot.at[:, other], foot_all.at[1], partner),
     ]
     pairs = (
@@ -163,19 +166,12 @@
     )
     for at, (src, dst) in enumerate(pairs):
         fixed.append(remote(f"m{at}", 0, src, dst, partner))
-    local_flux = pltpu.make_async_copy(flux.at[:, mine], gath.at[z, y, x, my_rows, :], local_sem.at[0])
+    local_flux = pltpu.make_async_copy(flux.at[:, :, mine], staged.at[0], local_sem.at[0])
     local_foot = pltpu.make_async_copy(foot.at[:, mine], foot_all.at[0], local_sem.at[1])
     local_flux.start()
     for copy in fixed:
         copy.start()
     local_foot.start()
-
-    def nearest(k):
-        picked = z
-        for place in range(depth):
-            order = sorted(range(depth), key=lambda other_z: (abs(other_z - place), other_z))
-            picked = jnp.where(z == place, order[k], picked)
-        return picked
 
     def gather_z(zz, upward):
         block = gath.at[zz, y, x]
@@ -205,7 +201,7 @@
             jnp.where(hot, to_col(swin_r[...].astype(jnp.float32)), 0.0), axis=0, keepdims=True
         ) - lag_r[...].astype(jnp.float32)
         window = window.astype(jnp.int32)
-        own = to_row(owner_r[...].astype(jnp.float32)).astype(jnp.int32)
+        own = owner_r[...]
         late = jnp.where(window >= windows, 1, 0)
         chip = ((own >> 2) * 2 + late) * 2 + ((own >> 1) & 1)
         inner = (own & 1) * rows_dev + (window - late * windows) * tile_dev + tile_r[...]
@@ -220,6 +216,18 @@
 
     local_flux.wait()
     fixed[0].wait_recv()
+
+    def place(step, carry):
+        cells = pl.ds(pl.multiple_of(step * tile_cells, tile_cells), tile_cells)
+        own_rows = staged[0, :, :, cells].reshape(rows_dev, tile_cells)
+        other_rows = staged[1, :, :, cells].reshape(rows_dev, tile_cells)
+        gath[z, y, x, :, cells] = jnp.concatenate(
+            [jnp.where(core == 0, own_rows, other_rows), jnp.where(core == 0, other_rows, own_rows)],
+            axis=0,
+        )
+        return carry
+
+    lax.fori_loop(0, half // tile_cells, place, 0)
     total = [jnp.zeros((entries, 1), jnp.float32)] * 2
     id_cols = [None, None]
     for k in range(depth + 2):
@@ -275,27 +283,16 @@
     vals = remote("vals", 0, val_send, val_recv, partner)
     vals.start()
     vals.wait_recv()
+    resids = []
     for h in range(2):
         value = val_send[h] + val_recv[1 - h]
         modeled = to_row(jnp.sum(jnp.where(hots[h], value, 0.0), axis=1, keepdims=True))
         if h == 0:
             modeled_out[...] = modeled
         residual = sets[h][6][...] * (modeled - sets[h][5][...])
-        resid = to_col(
-            jnp.sum(jnp.where(hots[h], to_col(residual), 0.0), axis=0, keepdims=True)
+        resids.append(
+            to_col(jnp.sum(jnp.where(hots[h], to_col(residual), 0.0), axis=0, keepdims=True))
         )
-
-        def scale(step, carry):
-            cells = pl.ds(pl.multiple_of(step * tile_cells, tile_cells), tile_cells)
-            scaled = resid * foot_all[h, :, cells].astype(jnp.float32)
-            contrib[pl.ds(h * entries, entries), cells] = scaled.astype(jnp.bfloat16)
-            return carry
-
-        lax.fori_loop(0, half // tile_cells, scale, 0)
-
-    def partial(rows, cells):
-        pick = jnp.where(row_ids[...] == rows, 1.0, 0.0).astype(jnp.bfloat16)
-        return jnp.dot(pick, contrib[:, cells], preferred_element_type=jnp.float32)
 
     def over(offset, body):
         def step_body(step, carry):
@@ -305,9 +302,15 @@
 
         lax.fori_loop(0, quarter // tile_back, step_body, 0)
 
-    def rows_of(zz, yy, xx):
-        base = ((zz * 2 + yy) * 2 + xx) * rows_chip
-        return lax.broadcasted_iota(jnp.int32, (rows_chip, 2 * entries), 0) + base
+    def scale(near, cells):
+        for h in range(2):
+            scaled = resids[h] * foot_all[h, :, cells].astype(jnp.float32)
+            contrib[pl.ds(h * entries, entries), cells] = scaled.astype(jnp.bfloat16)
+
+    def pick_rows(*bases):
+        own = lax.broadcasted_iota(jnp.int32, (rows_chip, 2 * entries), 0)
+        rows = jnp.concatenate([own + base for base in bases], axis=0)
+        return jnp.where(row_ids[...] == rows, 1.0, 0.0).astype(jnp.bfloat16)
 
     def scatter_1x(zz):
         return remote("s1x", zz, t1x.at[zz], a1x.at[zz], xn)
@@ -321,46 +324,67 @@
     def scatter_2y(zz):
         return remote("s2y", zz, t2y.at[zz], a2y.at[zz], yn)
 
-    def scatter_z(zz, part, upward):
+    def scatter_z(zz, part):
         cells = high if part else low
-        kind = ("up" if upward else "down") + str(part)
-        into = zup if upward else zdown
-        return remote(kind, zz, zsum.at[zz, :, :, cells], into.at[zz, :, :, cells], zu if upward else zd)
+        kind = KIND[f"z{part}"]
+        return pltpu.make_async_remote_copy(
+            src_ref=tz.at[zz, :, cells],
+            dst_ref=az.at[z, :, cells],
+            send_sem=send_sem.at[kind, zz],
+            recv_sem=recv_sem.at[kind, z],
+            device_id=along_z(zz),
+            device_id_type=pl.DeviceIdType.MESH,
+        )
+
+    def from_z(zz, part):
+        cells = high if part else low
+        kind = KIND[f"z{part}"]
+        return pltpu.make_async_remote_copy(
+            src_ref=tz.at[zz, :, cells],
+            dst_ref=az.at[zz, :, cells],
+            send_sem=send_sem.at[kind, zz],
+            recv_sem=recv_sem.at[kind, zz],
+            device_id=along_z(zz),
+            device_id_type=pl.DeviceIdType.MESH,
+        )
 
     def finish(part, far):
         cells = high if part else low
         into = pl.ds(pl.multiple_of(core * half + part * quarter, quarter), quarter)
         if far:
-            return remote("fin", part, zsum.at[z, 1 - core, :, cells], out.at[:, into], partner)
-        return pltpu.make_async_copy(zsum.at[z, core, :, cells], out.at[:, into], local_sem.at[part])
-
-    def first(zz):
-        row_x = jnp.concatenate([rows_of(zz, 0, 1 - x), rows_of(zz, 1, 1 - x)], axis=0)
-        row_y = jnp.concatenate([rows_of(zz, 1 - y, 0), rows_of(zz, 1 - y, 1)], axis=0)
-
-        def for_x(near, cells):
-            t1x[zz, :, :, near] = (
-                partial(row_x, cells).astype(jnp.bfloat16).reshape(2, rows_chip, tile_back)
-            )
-
-        def for_y(near, cells):
-            t1y[zz, :, :, near] = (
-                partial(row_y, cells).astype(jnp.bfloat16).reshape(2, rows_chip, tile_back)
-            )
-
-        over(0, for_x)
+            return remote("fin", part, zsum.at[1 - core, :, cells], out.at[:, into], partner)
+        return pltpu.make_async_copy(zsum.at[core, :, cells], out.at[:, into], local_sem.at[part])
+
+    def first(zz, fresh):
+        def chip(yy, xx):
+            return ((zz * 2 + yy) * 2 + xx) * rows_chip
+
+        def run(offset, bases, sent, kept):
+            pick = pick_rows(*bases)
+
+            def body(near, cells):
+                summed = jnp.dot(pick, contrib[:, cells], preferred_element_type=jnp.float32)
+                summed = summed.reshape(2, 2, rows_chip, tile_back)
+                sent[zz, :, :, near] = summed[0].astype(jnp.bfloat16)
+                kept[zz, :, :, near] = summed[1]
+
+            if fresh:
+                over(offset, scale)
+            over(offset, body)
+
+        run(0, (chip(0, 1 - x), chip(1, 1 - x), chip(0, x), chip(1, x)), t1x, keep_x)
         scatter_1x(zz).start()
-        over(quarter, for_y)
+        run(quarter, (chip(1 - y, 0), chip(1 - y, 1), chip(y, 0), chip(y, 1)), t1y, keep_y)
         scatter_1y(zz).start()
 
     def second(zz):
         def for_y(near, cells):
             got = a1x[zz, 1 - y, :, near].astype(jnp.float32)
-            t2y[zz, :, near] = (partial(rows_of(zz, 1 - y, x), cells) + got).astype(jnp.bfloat16)
+            t2y[zz, :, near] = (keep_x[zz, 1 - y, :, near] + got).astype(jnp.bfloat16)
 
         def for_x(near, cells):
             got = a1y[zz, 1 - x, :, near].astype(jnp.float32)
-            t2x[zz, :, near] = (partial(rows_of(zz, y, 1 - x), cells) + got).astype(jnp.bfloat16)
+            t2x[zz, :, near] = (keep_y[zz, 1 - x, :, near] + got).astype(jnp.bfloat16)
 
         scatter_1x(zz).wait_recv()
         over(0, for_y)
@@ -369,45 +393,42 @@
         over(quarter, for_x)
         scatter_2x(zz).start()
 
-    def third(zz, part):
-        def gather_sum(near, cells):
+    def third(zz, part, last):
+        def plane_sum(near):
             if part:
-                got = a1y[zz, x, :, near].astype(jnp.float32) + a2x[zz, :, near].astype(jnp.float32)
-            else:
-                got = a1x[zz, y, :, near].astype(jnp.float32) + a2y[zz, :, near].astype(jnp.float32)
-            summed = partial(rows_of(zz, y, x), cells) + got
-            zsum[zz, :, :, cells] = summed.reshape(2, rows_dev, tile_back)
-
-        def add_from(source):
-            def body(near, cells):
-                zsum[zz, :, :, cells] = zsum[zz, :, :, cells] + source[zz, :, :, cells]
-
-            return body
+                return keep_y[zz, x, :, near] + (
+                    a1y[zz, x, :, near].astype(jnp.float32) + a2x[zz, :, near].astype(jnp.float32)
+                )
+            return keep_x[zz, y, :, near] + (
+                a1x[zz, y, :, near].astype(jnp.float32) + a2y[zz, :, near].astype(jnp.float32)
+            )
+
+        def send_on(near, cells):
+            tz[zz, :, cells] = plane_sum(near).astype(jnp.bfloat16)
+
+        def sum_up(near, cells):
+            summed = plane_sum(near)
+            for k in range(1, depth):
+                summed = summed + az[nearest(k), :, cells].astype(jnp.float32)
+            zsum[:, :, cells] = summed.reshape(2, rows_dev, tile_back)
 
         (scatter_2x if part else scatter_2y)(zz).wait_recv()
-        over(part * quarter, gather_sum)
-
-        @pl.when((zz >= z) & has_down)
-        def _():
-            scatter_z(zz, part, True).wait_recv()
-            over(part * quarter, add_from(zup))
-
-        @pl.when((zz <= z) & has_up)
-        def _():
-            scatter_z(zz, part, False).wait_recv()
-            over(part * quarter, add_from(zdown))
-
-        pl.when(zz > z)(lambda: scatter_z(zz, part, True).start())
-        pl.when(zz < z)(lambda: scatter_z(zz, part, False).start())
+        if last:
+            for k in range(1, depth):
+                from_z(nearest(k), part).wait_recv()
+            over(part * quarter, sum_up)
+        else:
+            over(part * quarter, send_on)
+            scatter_z(zz, part).start()
 
     for k in range(depth + 2):
         if k < depth:
-            first(nearest(depth - 1 - k))
+            first(nearest(depth - 1 - k), k == 0)
         if 1 <= k <= depth:
             second(nearest(depth - k))
         if k >= 2:
             for part in range(2):
-                third(nearest(depth + 1 - k), part)
+                third(nearest(depth + 1 - k), part, k == depth + 1)
                 if k == depth + 1:
                     finish(part, True).start()
                     finish(part, False).start()
@@ -417,6 +438,9 @@
     for copy in fixed:
         copy.wait_send()
     vals.wait_send()
+    for k in range(1, depth):
+        for part in range(2):
+            scatter_z(nearest(k), part).wait_send()
 
     def drain(zz, carry):
         pl.when((zz <= z) & has_up)(lambda: gather_z(zz, True).wait_send())
@@ -426,9 +450,6 @@
             scatter_1x, scatter_1y, scatter_2x, scatter_2y,
         ):
             copy(zz).wait_send()
-        for part in range(2):
-            pl.when(zz > z)(lambda: scatter_z(zz, part, True).wait_send())
-            pl.when(zz < z)(lambda: scatter_z(zz, part, False).wait_send())
         return carry
 
     lax.fori_loop(0, depth, drain, 0)
@@ -455,7 +476,7 @@
             pltpu.VMEM((2, entries, half), bf),
             pltpu.VMEM((2 * entries, half), bf),
             pltpu.VMEM((depth, 2, 2, rows_chip, half), bf),
-            pltpu.VMEM((entries, 1), i32),
+            pltpu.VMEM((1, entries), i32),
             pltpu.VMEM((1, entries), i32),
             pltpu.VMEM((1, entries), i32),
             pltpu.VMEM((1, entries), i32),
@@ -465,15 +486,18 @@
             pltpu.VMEM((2, 1, entries), f32),
             pltpu.VMEM((2, 1, entries), f32),
             pltpu.VMEM((1, 2 * entries), i32),
+            pltpu.VMEM((2, windows, tile_dev, half), bf),
             *[pltpu.VMEM((depth, 2, rows_chip, quarter), bf)] * 4,
             *[pltpu.VMEM((depth, rows_chip, quarter), bf)] * 4,
-            *[pltpu.VMEM((depth, 2, rows_dev, half), f32)] * 3,
+            *[pltpu.VMEM((depth, 2, rows_chip, quarter), f32)] * 2,
+            *[pltpu.VMEM((depth, rows_chip, half), bf)] * 2,
+            pltpu.VMEM((2, rows_dev, half), f32),
             pltpu.SemaphoreType.DMA((len(KINDS), depth)),
             pltpu.SemaphoreType.DMA((len(KINDS), depth)),
             pltpu.SemaphoreType.DMA((2,)),
         ],
         compiler_params=pltpu.CompilerParams(collective_id=0, has_side_effects=True),
-    )(flux.reshape(rows_dev, cells), footprint, owner, tile, lag, sounding, swin, observed, weight)
+    )(flux, footprint, owner.reshape(1, entries), tile, lag, sounding, swin, observed, weight)
     return modeled, gradient.reshape(windows, tile_dev, cells)
 
 

time: 122 us -> 102 us (0.84)
  Pallas kernels: 115 us -> 97.9 us
  local copies, waits for them, and re-layouts: 6.2 us -> 3.09 us
    pallas_call x1, Pallas kernels: 115 us -> 97.9 us  [per_chip(): pl.pallas_call(functools.partial(chip_kernel, depth, windows, tile_dev),...]
    reshape x1 -> x0, local copies, waits for them, and re-layouts: 1.72 us -> none  [per_chip(): flux.reshape(rows_dev, cells)]
    unnamed x2 -> x1, local copies, waits for them, and re-layouts: 2.5 us -> 1.11 us
where the time goes in v2:
time: 102 us
  Pallas kernels  97.9 us (96%)
  local copies, waits for them, and re-layouts  3.09 us (3%)
    pallas_call x1, Pallas kernels, per_chip(): pl.pallas_call(functools.partial(chip_kernel, depth, windows, tile_dev),...  97.9 us

profile of v2, /device:TPU:0, one launch (start us, length us, event | category | flops | bytes accessed | tf_op | source)
XLA Modules:
  0.0 101.7 jit_solution(1669270200129761559)
XLA Ops:
  0.6 97.9 %shard_map.104 = (f32[1,16]{1,0:T(1,128)}, f32[8,16384]{1,0:T(8,128)}) custom-call(bf16[2,4,16384]{2,1,0:T(4,128)(2,1)} %flux.1, bf16[64,16384]{1,0:T(8,128)(2,1)} %foot.1, s32[1,64]{1,0:T(1,128)} %bitcast.1, s32[1,64]{1,0:T(1,128)} %tile.1, s32[1,64]{1,0:T(1,128)} %lag.1, s32[1,64]{1,0:T(1,128)} %sounding.1, s32[1,16]{1,0:T(1,128)} %swin.1, ...), custom_call_target="tpu_custom_call" | custom-call | tf_op jit(solution)/shard_map/pallas_call | solution.py:467
  98.6 2.0 %reshape.11 = f32[2,4,16384]{2,1,0:T(4,128)} reshape(f32[8,16384]{1,0:T(8,128)} %get-tuple-element.5) | data formatting | bytes 1048576 | tf_op jit(solution)/shard_map/reshape | solution.py:501
  100.6 1.1 %copy.12 = f32[1,16]{1,0:T(1,128)} copy(f32[1,16]{1,0:T(1,128)} %get-tuple-element.8) | data formatting | bytes 128

commit v3 on v2

--- a/solution.py
+++ b/solution.py
@@ -79,7 +79,7 @@
 
 KINDS = (
     "foot", "flux", "m0", "m1", "m2", "m3", "m4", "m5", "m6", "vals",
-    "gup", "gdown", "g1x", "g1y", "g2x", "g2y",
+    "gup0", "gup1", "gup2", "gdown0", "gdown1", "gdown2", "g1x", "g1y", "g2x", "g2y",
     "s1x", "s1y", "s2x", "s2y", "z0", "z1", "fin",
 )
 KIND = {name: at for at, name in enumerate(KINDS)}
@@ -110,6 +110,7 @@
     rows_dev = windows * tile_dev
     rows_chip = 2 * rows_dev
     rows_plane = 4 * rows_chip
+    extra = quarter // 2048 * 384
     tile_cells = min(1024, quarter)
     tile_back = min(1024, quarter)
     y = lax.axis_index("tm")
@@ -135,11 +136,18 @@
     def along_z(zz):
         return (y, o + 4 * (zz - z))
 
+    mine = pl.ds(pl.multiple_of(core * half, half), half)
+    other = pl.ds(pl.multiple_of((1 - core) * half, half), half)
+    low, high = pl.ds(0, quarter), pl.ds(quarter, quarter)
+    local_flux = pltpu.make_async_copy(flux.at[:, :, mine], staged.at[0], local_sem.at[0])
+    local_foot = pltpu.make_async_copy(foot.at[:, mine], foot_all.at[0], local_sem.at[1])
     barrier = pltpu.get_barrier_semaphore()
     for device in (partner, xn, yn, *(along_z(nearest(k)) for k in range(1, depth))):
         pl.semaphore_signal(
             barrier, inc=1, device_id=device, device_id_type=pl.DeviceIdType.MESH
         )
+    local_flux.start()
+    local_foot.start()
     pl.semaphore_wait(barrier, 2 + depth)
 
     def remote(kind, at, src, dst, device):
@@ -152,10 +160,6 @@
             device_id_type=pl.DeviceIdType.MESH,
         )
 
-    mine = pl.ds(pl.multiple_of(core * half, half), half)
-    other = pl.ds(pl.multiple_of((1 - core) * half, half), half)
-    low, high = pl.ds(0, quarter), pl.ds(quarter, quarter)
-
     fixed = [
         remote("flux", 0, flux.at[:, :, other], staged.at[1], partner),
         remote("foot", 0, foot.at[:, other], foot_all.at[1], partner),
@@ -166,31 +170,49 @@
     )
     for at, (src, dst) in enumerate(pairs):
         fixed.append(remote(f"m{at}", 0, src, dst, partner))
-    local_flux = pltpu.make_async_copy(flux.at[:, :, mine], staged.at[0], local_sem.at[0])
-    local_foot = pltpu.make_async_copy(foot.at[:, mine], foot_all.at[0], local_sem.at[1])
-    local_flux.start()
     for copy in fixed:
         copy.start()
-    local_foot.start()
-
-    def gather_z(zz, upward):
-        block = gath.at[zz, y, x]
-        return remote("gup" if upward else "gdown", zz, block, block, zu if upward else zd)
-
-    def gather_1x(zz):
-        block = gath.at[zz, y, x, :, low]
+
+    def gather_z(zz, part, upward):
+        cells = (
+            pl.ds(0, quarter - extra),
+            pl.ds(quarter + extra, quarter - extra),
+            pl.ds(quarter - extra, 2 * extra),
+        )[part]
+        block = gath.at[zz, :, :, :, cells] if part == 2 else gath.at[zz, y, x, :, cells]
+        kind = ("gup" if upward else "gdown") + str(part)
+        return remote(kind, zz, block, block, zu if upward else zd)
+
+    def send_z(zz, parts):
+        for part in parts:
+            pl.when((zz <= z) & has_up)(lambda: gather_z(zz, part, True).start())
+            pl.when((zz >= z) & has_down)(lambda: gather_z(zz, part, False).start())
+
+    def take_z(zz, parts):
+        for part in parts:
+            pl.when(zz < z)(lambda: gather_z(zz, part, True).wait_recv())
+            pl.when(zz > z)(lambda: gather_z(zz, part, False).wait_recv())
+
+    def low_of(own):
+        return low if own else pl.ds(0, quarter - extra)
+
+    def high_of(own):
+        return high if own else pl.ds(quarter + extra, quarter - extra)
+
+    def gather_1x(zz, own):
+        block = gath.at[zz, y, x, :, low_of(own)]
         return remote("g1x", zz, block, block, xn)
 
-    def gather_1y(zz):
-        block = gath.at[zz, y, x, :, high]
+    def gather_1y(zz, own):
+        block = gath.at[zz, y, x, :, high_of(own)]
         return remote("g1y", zz, block, block, yn)
 
-    def gather_2x(zz):
-        block = gath.at[zz, :, x, :, high]
+    def gather_2x(zz, own):
+        block = gath.at[zz, :, x, :, high_of(own)]
         return remote("g2x", zz, block, block, xn)
 
-    def gather_2y(zz):
-        block = gath.at[zz, y, :, :, low]
+    def gather_2y(zz, own):
+        block = gath.at[zz, y, :, :, low_of(own)]
         return remote("g2y", zz, block, block, yn)
 
     def fields(refs):
@@ -228,58 +250,83 @@
         return carry
 
     lax.fori_loop(0, half // tile_cells, place, 0)
-    total = [jnp.zeros((entries, 1), jnp.float32)] * 2
-    id_cols = [None, None]
-    for k in range(depth + 2):
-        if k < depth:
-            zz = nearest(k)
-            if k > 0:
-                pl.when(zz < z)(lambda: gather_z(zz, True).wait_recv())
-                pl.when(zz > z)(lambda: gather_z(zz, False).wait_recv())
-            pl.when((zz <= z) & has_up)(lambda: gather_z(zz, True).start())
-            pl.when((zz >= z) & has_down)(lambda: gather_z(zz, False).start())
-            gather_1x(zz).start()
-            gather_1y(zz).start()
-        if k == 1:
-            for copy in fixed[1:]:
-                copy.wait_recv()
-            local_foot.wait()
-            hots[1], ids[1] = fields(sets[1])
-            id_cols = [to_col(i.astype(jnp.float32)).astype(jnp.int32) for i in ids]
-            row_ids[...] = jnp.concatenate(ids, axis=1)
-        if 1 <= k <= depth:
-            zz = nearest(k - 1)
-            gather_1x(zz).wait_recv()
-            gather_1y(zz).wait_recv()
-            gather_2x(zz).start()
-            gather_2y(zz).start()
-        if k >= 2:
-            zz = nearest(k - 2)
-            gather_2x(zz).wait_recv()
-            gather_2y(zz).wait_recv()
-
-            def dots(step, acc):
-                cells = pl.ds(pl.multiple_of(step * tile_cells, tile_cells), tile_cells)
-                block = gath[zz, :, :, :, cells].reshape(rows_plane, tile_cells)
-                return tuple(
-                    acc[h]
-                    + lax.dot_general(
-                        foot_all[h, :, cells], block, (((1,), (1,)), ((), ())),
-                        preferred_element_type=jnp.float32,
-                    )
-                    for h in range(2)
-                )
-
-            zero = jnp.zeros((entries, rows_plane), jnp.float32)
-            acc = lax.fori_loop(0, half // tile_cells, dots, (zero, zero))
-            lanes = lax.broadcasted_iota(jnp.int32, (entries, rows_plane), 1) + zz * rows_plane
-            for h in range(2):
-                total[h] = total[h] + jnp.sum(
-                    jnp.where(id_cols[h] == lanes, acc[h], 0.0), axis=1, keepdims=True
-                )
+    def arrive(k):
+        zz = nearest(k)
+        if k > 0:
+            take_z(zz, (0, 1))
+        send_z(zz, (0, 1))
+        gather_1x(zz, k == 0).start()
+        gather_1y(zz, k == 0).start()
+
+    def widen(k):
+        zz = nearest(k)
+        gather_1x(zz, k == 0).wait_recv()
+        gather_1y(zz, k == 0).wait_recv()
+        gather_2x(zz, k == 0).start()
+        gather_2y(zz, k == 0).start()
+
+    def complete(k):
+        zz = nearest(k)
+        gather_2x(zz, k == 0).wait_recv()
+        gather_2y(zz, k == 0).wait_recv()
+
+    def spread(k):
+        zz = nearest(k)
+        if k > 0:
+            take_z(zz, (2,))
+        send_z(zz, (2,))
+
+    def values(k, total, ids_col):
+        zz = nearest(k)
+
+        def dots(step, acc):
+            cells = pl.ds(pl.multiple_of(step * quarter, quarter), quarter)
+            return acc + lax.dot_general(
+                foot_all[:, :, cells].reshape(2 * entries, quarter),
+                gath[zz, :, :, :, cells].reshape(rows_plane, quarter),
+                (((1,), (1,)), ((), ())),
+                preferred_element_type=jnp.float32,
+            )
+
+        acc = lax.fori_loop(
+            0, half // quarter, dots, jnp.zeros((2 * entries, rows_plane), jnp.float32)
+        )
+        lanes = lax.broadcasted_iota(jnp.int32, (2 * entries, rows_plane), 1) + zz * rows_plane
+        return total + jnp.sum(jnp.where(ids_col == lanes, acc, 0.0), axis=1, keepdims=True)
+
+    arrive(0)
+    widen(0)
+    total = jnp.zeros((2 * entries, 1), jnp.float32)
+    arrive(1)
+    complete(0)
+    spread(0)
+    for copy in fixed[1:]:
+        copy.wait_recv()
+    local_foot.wait()
+    hots[1], ids[1] = fields(sets[1])
+    row_ids[...] = jnp.concatenate(ids, axis=1)
+    ids_col = jnp.concatenate(
+        [to_col(i.astype(jnp.float32)).astype(jnp.int32) for i in ids], axis=0
+    )
+    total = values(0, total, ids_col)
+    for k in range(2, depth):
+        arrive(k)
+        if k < depth - 1:
+            widen(k - 1)
+    widen(max(depth - 2, 1))
+    if depth > 2:
+        widen(depth - 1)
+    spread(1)
+    if depth > 2:
+        spread(2)
+    for k in range(1, depth):
+        complete(k)
+        if k > 2:
+            spread(k)
+        total = values(k, total, ids_col)
 
     for h in range(2):
-        val_send[h] = to_row(total[h])
+        val_send[h] = to_row(total[h * entries : (h + 1) * entries])
     vals = remote("vals", 0, val_send, val_recv, partner)
     vals.start()
     vals.wait_recv()
@@ -421,17 +468,25 @@
             over(part * quarter, send_on)
             scatter_z(zz, part).start()
 
-    for k in range(depth + 2):
-        if k < depth:
-            first(nearest(depth - 1 - k), k == 0)
-        if 1 <= k <= depth:
+    def leave(k):
+        for part in range(2):
+            third(nearest(depth - 1 - k), part, k == depth - 1)
+            if k == depth - 1:
+                finish(part, True).start()
+                finish(part, False).start()
+
+    for k in range(depth - 1):
+        first(nearest(depth - 1 - k), k == 0)
+        if k > 0:
             second(nearest(depth - k))
-        if k >= 2:
-            for part in range(2):
-                third(nearest(depth + 1 - k), part, k == depth + 1)
-                if k == depth + 1:
-                    finish(part, True).start()
-                    finish(part, False).start()
+        if k > 1:
+            leave(k - 2)
+    second(nearest(1))
+    first(nearest(0), False)
+    for k in range(max(depth - 3, 0), depth - 1):
+        leave(k)
+    second(nearest(0))
+    leave(depth - 1)
     for part in range(2):
         finish(part, False).wait()
         finish(part, True).wait()
@@ -443,16 +498,17 @@
             scatter_z(nearest(k), part).wait_send()
 
     def drain(zz, carry):
-        pl.when((zz <= z) & has_up)(lambda: gather_z(zz, True).wait_send())
-        pl.when((zz >= z) & has_down)(lambda: gather_z(zz, False).wait_send())
-        for copy in (
-            gather_1x, gather_1y, gather_2x, gather_2y,
-            scatter_1x, scatter_1y, scatter_2x, scatter_2y,
-        ):
+        for part in range(3):
+            pl.when((zz <= z) & has_up)(lambda: gather_z(zz, part, True).wait_send())
+            pl.when((zz >= z) & has_down)(lambda: gather_z(zz, part, False).wait_send())
+        for copy in (scatter_1x, scatter_1y, scatter_2x, scatter_2y):
             copy(zz).wait_send()
         return carry
 
     lax.fori_loop(0, depth, drain, 0)
+    for k in range(depth):
+        for copy in (gather_1x, gather_1y, gather_2x, gather_2y):
+            copy(nearest(k), k == 0).wait_send()
 
 
 def per_chip(depth, flux, footprint, owner, tile, lag, sounding, swin, observed, weight):
@@ -520,7 +576,7 @@
     def routed(flux, *rest):
         rows = flux.shape[0] * flux.shape[1] * times * places
         fits = rows * flux.shape[2] * 8 <= 40 * 2**20
-        plain = flux.shape[0] * flux.shape[1] % 8 == 0 and flux.shape[2] % 2048 == 0
+        plain = flux.shape[0] * flux.shape[1] % 8 == 0 and flux.shape[2] % 8192 == 0
         body = functools.partial(per_chip, depth) if grouped and fits and plain else per_device
         return body(flux, *rest)
 

time: 102 us -> 98.1 us (0.962)
  Pallas kernels: 97.9 us -> 94.2 us
    pallas_call x1, Pallas kernels: 97.9 us -> 94.2 us  [per_chip(): pl.pallas_call(functools.partial(chip_kernel, depth, windows, tile_dev),...]
where the time goes in v3:
time: 98.1 us; the launch traced here: 98 us
  Pallas kernels  94.2 us (96%)
  local copies, waits for them, and re-layouts  3.09 us (3%)
    pallas_call x1, Pallas kernels, per_chip(): pl.pallas_call(functools.partial(chip_kernel, depth, windows, tile_dev),...  94.2 us
    reshape x1, local copies, waits for them, and re-layouts, per_chip(): return (modeled, gradient.reshape(windows, tile_dev, cells))  1.98 us

profile of v3, /device:TPU:0, one launch (start us, length us, event | category | flops | bytes accessed | tf_op | source)
XLA Modules:
  0.0 98.0 jit_solution(480612282501098403)
XLA Ops:
  0.6 94.2 %shard_map.104 = (f32[1,16]{1,0:T(1,128)}, f32[8,16384]{1,0:T(8,128)}) custom-call(bf16[2,4,16384]{2,1,0:T(4,128)(2,1)} %flux.1, bf16[64,16384]{1,0:T(8,128)(2,1)} %foot.1, s32[1,64]{1,0:T(1,128)} %bitcast.1, s32[1,64]{1,0:T(1,128)} %tile.1, s32[1,64]{1,0:T(1,128)} %lag.1, s32[1,64]{1,0:T(1,128)} %sounding.1, s32[1,16]{1,0:T(1,128)} %swin.1, ...), custom_call_target="tpu_custom_call" | custom-call | tf_op jit(solution)/shard_map/pallas_call | solution.py:523
  94.9 2.0 %reshape.11 = f32[2,4,16384]{2,1,0:T(4,128)} reshape(f32[8,16384]{1,0:T(8,128)} %get-tuple-element.5) | data formatting | bytes 1048576 | tf_op jit(solution)/shard_map/reshape | solution.py:557
  96.9 1.1 %copy.12 = f32[1,16]{1,0:T(1,128)} copy(f32[1,16]{1,0:T(1,128)} %get-tuple-element.8) | data formatting | bytes 128
